TPU v7x, 32 devices: a whole 2x2x4 slice. The times are simulated.
32 devices in a mesh: wide: 8 (over y, x, core), narrow: 4 (over z).
Axes of the slice: x: 2, y: 2, z: 4, core: 2. Of those that a mesh axis runs over, the one named last changes fastest.
Arguments:
- activity: bfloat16 [32, 8, 512, 512], P(('wide', 'narrow')), may hold values from 0 to 1
- tile_coords: int32 [32, 2], replicated, may hold values from 0 to 7, as said below
- user_owner: int32 [8], replicated, may hold values from 0 to 7, each once
- item_owner: int32 [8], replicated, may hold values from 0 to 7, each once
- user_factor: float32 [4096, 256], P('wide', 'narrow'), may hold values from 0 to 1
- item_factor: float32 [4096, 256], P('wide', 'narrow'), may hold values from 0 to 1
- time_factor: float32 [8, 256], replicated, may hold values from 0.0003 to 0.003
- user_dual: float32 [4096, 256], P('wide', 'narrow'), may hold values from -1.8 to 1.8
- item_dual: float32 [4096, 256], P('wide', 'narrow'), may hold values from -1.8 to 1.8
Outputs:
- new_users: float32 [4096, 256], P('wide', 'narrow')
- new_items: float32 [4096, 256], P('wide', 'narrow')
- new_user_dual: float32 [4096, 256], P('wide', 'narrow')
- new_item_dual: float32 [4096, 256], P('wide', 'narrow')
Inputs may be any that keep to these rules, and one draw needn't show every extreme that they name: `tile_coords`: no pair of blocks appears twice. `user_owner`: each stored row block holds exactly one user block. `item_owner`: each stored row block holds exactly one item block.
All inputs are finite; a program needn't handle non-finite values.
Results may differ from a plain program's by a relative error of at most 0.0017.
The roundings to bfloat16 on the way count: a program that leaves them out, or rounds other values in their place, can miss the bound.
Values may be sent and summed in bfloat16 or wider, within the bound.
No kernel may reach another device: no remote copies, remote signals or barrier semaphores. Data moves between devices by JAX's collectives and lax.ppermute only.
A program may use at most 64 MiB of HBM per device.

v0:
```python
import jax
import jax.numpy as jnp
from jax import lax
from jax.sharding import PartitionSpec as P

RANK = 256
BLOCK = 512
PASSES = 2


def locate(owner, wanted_blocks):
    everyone = jnp.arange(owner.shape[0], dtype=jnp.int32)
    chosen = jnp.where(everyone[None, :] == wanted_blocks[:, None], owner[None, :], 0)
    return jnp.sum(chosen, axis=1)


def fetch_rows(factor, wanted):
    lowered = factor.astype(jnp.bfloat16)
    width = factor.shape[1]
    slots = wanted.shape[0]
    initial = jnp.zeros((slots, BLOCK, width), jnp.bfloat16)
    portion = lax.all_gather(lowered, "wide", axis=0, tiled=True)
    count_blocks = portion.shape[0] // BLOCK
    shaped = portion.reshape(count_blocks, BLOCK, width)
    first = jnp.int32(0) // BLOCK
    onehot = (wanted[:, None] == first + jnp.arange(count_blocks, dtype=jnp.int32)[None, :]).astype(
        jnp.bfloat16
    )
    picked = jnp.einsum("jq,qrc->jrc", onehot, shaped, preferred_element_type=jnp.float32)
    gathered = initial + picked.astype(jnp.bfloat16)
    return lax.all_to_all(gathered, "narrow", split_axis=0, concat_axis=2, tiled=True)


def tile_sums(activity, fetched, time_factor, forward):
    khatri = (fetched.astype(jnp.float32)[:, None] * time_factor[None, :, None, :]).astype(
        jnp.bfloat16
    )
    if forward:
        return jnp.einsum("tkij,tkjr->tir", activity, khatri, preferred_element_type=jnp.float32)
    return jnp.einsum("tkij,tkir->tjr", activity, khatri, preferred_element_type=jnp.float32)


def owner_sums(partial_value, targets, owned):
    received = lax.all_to_all(partial_value, "narrow", split_axis=2, concat_axis=0, tiled=True)
    width = received.shape[2]
    count_blocks = owned * lax.axis_size("wide") // BLOCK
    onehot = (jnp.arange(count_blocks, dtype=jnp.int32)[:, None] == targets[None, :]).astype(
        jnp.float32
    )
    placed = jnp.einsum("qj,jrc->qrc", onehot, received, precision=lax.Precision.HIGHEST)
    return lax.psum_scatter(
        placed.reshape(owned * lax.axis_size("wide"), width),
        "wide",
        scatter_dimension=0,
        tiled=True,
    )


def joint_gram(other_rows, time_factor):
    local_gram = jnp.dot(other_rows.T, other_rows, precision=lax.Precision.HIGHEST)
    total = lax.psum(local_gram, ("wide", "narrow"))
    gram = total * jnp.dot(time_factor.T, time_factor, precision=lax.Precision.HIGHEST)
    penalty = jnp.trace(gram) / RANK
    identity = jnp.eye(RANK, dtype=jnp.float32)
    lower = jnp.linalg.cholesky(gram + penalty * identity)
    inverse = jax.scipy.linalg.cho_solve((lower, True), identity)
    return (penalty, inverse)


def update_rows(
    activity, other_cols, other_rows, factor, dual, wanted, targets, time_factor, forward, owned
):
    fetched = fetch_rows(other_cols, wanted)
    partial_value = tile_sums(activity, fetched, time_factor, forward)
    sums = owner_sums(partial_value, targets, owned)
    sums_rows = lax.all_to_all(sums, "narrow", split_axis=0, concat_axis=1, tiled=True)
    penalty, inverse = joint_gram(other_rows, time_factor)
    for _ in range(PASSES):
        target = jnp.dot(
            sums_rows + penalty * (factor + dual), inverse, precision=lax.Precision.HIGHEST
        )
        factor = jnp.maximum(target - dual, 0.0)
        dual = dual + factor - target
    factor_cols, dual_cols = (
        lax.all_to_all(factor, "narrow", split_axis=1, concat_axis=0, tiled=True),
        lax.all_to_all(dual, "narrow", split_axis=1, concat_axis=0, tiled=True),
    )
    return (factor_cols, dual_cols, factor)


def local(
    activity,
    tile_coords,
    user_owner,
    item_owner,
    user_factor,
    item_factor,
    time_factor,
    user_dual,
    item_dual,
):
    narrow_size = lax.axis_size("narrow")
    slots = narrow_size * activity.shape[0]
    group_coords = lax.dynamic_slice_in_dim(tile_coords, lax.axis_index("wide") * slots, slots, 0)
    user_pos = locate(user_owner, group_coords[:, 0])
    item_pos = locate(item_owner, group_coords[:, 1])
    owned = user_factor.shape[0]
    user_rows, udual_rows, item_rows, idual_rows = (
        lax.all_to_all(user_factor, "narrow", split_axis=0, concat_axis=1, tiled=True),
        lax.all_to_all(user_dual, "narrow", split_axis=0, concat_axis=1, tiled=True),
        lax.all_to_all(item_factor, "narrow", split_axis=0, concat_axis=1, tiled=True),
        lax.all_to_all(item_dual, "narrow", split_axis=0, concat_axis=1, tiled=True),
    )
    new_users, new_user_dual, fresh_rows = update_rows(
        activity,
        item_factor,
        item_rows,
        user_rows,
        udual_rows,
        item_pos,
        user_pos,
        time_factor,
        True,
        owned,
    )
    new_items, new_item_dual, _ = update_rows(
        activity,
        new_users,
        fresh_rows,
        item_rows,
        idual_rows,
        user_pos,
        item_pos,
        time_factor,
        False,
        owned,
    )
    return (new_users, new_items, new_user_dual, new_item_dual)


def solution(mesh):
    in_specs = (
        P(("wide", "narrow"), None, None, None),
        P(),
        P(),
        P(),
        P("wide", "narrow"),
        P("wide", "narrow"),
        P(),
        P("wide", "narrow"),
        P("wide", "narrow"),
    )
    out_specs = (P("wide", "narrow"), P("wide", "narrow"), P("wide", "narrow"), P("wide", "narrow"))
    return jax.shard_map(local, mesh=mesh, in_specs=in_specs, out_specs=out_specs, check_vma=False)
```

profile of v0, /device:TPU:0, one launch (start us, length us, event | category | flops | bytes accessed | tf_op | source)
XLA Modules:
  0.0 562.6 jit_solution(15027327676209226072)
XLA Ops:
  9.6 6.3 %all-to-all-start.3 = ((f32[4,128,64]{1,2,0:T(8,128)}), f32[4,128,64]{1,2,0:T(8,128)S(1)}, u32[]{:S(2)}, u32[]{:S(2)}) async-start(f32[4,128,64]{1,2,0:T(8,128)} %copy_bitcast_fusion.8), calls=%async_computation.4 | async-start | bytes 262144 | tf_op jit(solution)/shard_map/all_to_all | solution.py:111
  16.9 9.9 %all_gather.6 = bf16[4096,64]{0,1:T(8,128)(2,1)S(1)} all-gather(bf16[512,64]{0,1:T(8,128)(2,1)S(1)} %convert_element_type.70), channel_id=1, replica_groups=mesh['wide'=8,'narrow'=4] {'wide'}, dimensions={0}, use_global_device_ids=true | all-gather | bytes 589824 | tf_op jit(solution)/shard_map/all_gather | solution.py:22
  33.5 5.1 all-to-all-start.4
  39.7 5.3 all-to-all-done.4
  49.3 5.1 all-to-all-done.5
  57.8 116.1 %all-reduce.4.cloned.1.call-done = f32[256,256]{0,1:T(8,128)} async-done(((f32[256,256]{0,1:T(8,128)}), f32[256,256]{0,1:T(8,128)}) %all-reduce.4.cloned.1.call-update) | async-done | bytes 262160 | tf_op jit(solution)/shard_map/psum | solution.py:61
  176.8 11.7 %cholesky.130 = f32[128,128]{1,0:T(8,128)S(1)} custom-call(f32[128,128]{1,0:T(8,128)S(1)} %cholesky.194), custom_call_target="Cholesky" | custom-call | tf_op jit(solution)/shard_map/jit(cholesky)/cholesky | solution.py:65
  188.6 9.8 %custom-call.15 = f32[1,128,128]{1,2,0:T(8,128)S(1)} custom-call(f32[1,128,128]{2,1,0:T(8,128)S(1)} %get-tuple-element.59), custom_call_target="InvertDiagBlocksLowerTriangular" | custom-call | tf_op jit(solution)/shard_map/jit(cholesky)/cholesky | solution.py:65
  207.8 11.7 %cholesky.147 = f32[128,128]{1,0:T(8,128)S(1)} custom-call(f32[128,128]{1,0:T(8,128)S(1)} %convolution_subtract_fusion.5), custom_call_target="Cholesky" | custom-call | tf_op jit(solution)/shard_map/jit(cholesky)/cholesky | solution.py:65
  228.3 19.7 %custom-call.16 = f32[2,128,128]{1,2,0:T(8,128)S(1)} custom-call(f32[2,128,128]{2,1,0:T(8,128)S(1)} %get-tuple-element.20), custom_call_target="InvertDiagBlocksLowerTriangular" | custom-call | tf_op jit(solution)/shard_map/jit(_cho_solve)/triangular_solve | solution.py:66
  249.6 12.0 %reduce-scatter.3.cloned.1.call-done = f32[512,64]{0,1:T(8,128)} async-done(((f32[4096,64]{0,1:T(8,128)}), f32[512,64]{0,1:T(8,128)}) %reduce-scatter.3.cloned.1.call-update) | async-done | bytes 131088 | tf_op jit(solution)/shard_map/reduce_scatter | solution.py:51
  263.2 4.6 all-to-all-start.2
  268.1 5.7 %all-to-all-done.2 = f32[4,128,64]{1,2,0:T(8,128)S(1)} async-done(((f32[4,128,64]{1,2,0:T(8,128)}), f32[4,128,64]{1,2,0:T(8,128)S(1)}, u32[]{:S(2)}, u32[]{:S(2)}) %all-to-all-start.2) | async-done | bytes 131104 | tf_op jit(solution)/shard_map/all_to_all | solution.py:76
  287.9 122.6 %all-reduce.6.cloned.1.call-done = f32[256,256]{0,1:T(8,128)} async-done(((f32[256,256]{0,1:T(8,128)}), f32[256,256]{0,1:T(8,128)}) %all-reduce.6.cloned.1.call-update) | async-done | bytes 262160 | tf_op jit(solution)/shard_map/psum | solution.py:61
  413.6 10.0 %all_gather.7 = bf16[4096,64]{0,1:T(8,128)(2,1)S(1)} all-gather(bf16[512,64]{0,1:T(8,128)(2,1)S(1)} %get-tuple-element.40), channel_id=1, replica_groups=mesh['wide'=8,'narrow'=4] {'wide'}, dimensions={0}, use_global_device_ids=true | all-gather | bytes 589824 | tf_op jit(solution)/shard_map/all_gather | solution.py:22
  428.5 11.7 %cholesky.164 = f32[128,128]{1,0:T(8,128)S(1)} custom-call(f32[128,128]{1,0:T(8,128)S(1)} %cholesky.197), custom_call_target="Cholesky" | custom-call | tf_op jit(solution)/shard_map/jit(cholesky)/cholesky | solution.py:65
  440.3 9.8 %custom-call.17 = f32[1,128,128]{1,2,0:T(8,128)S(1)} custom-call(f32[1,128,128]{2,1,0:T(8,128)S(1)} %get-tuple-element.55), custom_call_target="InvertDiagBlocksLowerTriangular" | custom-call | tf_op jit(solution)/shard_map/jit(cholesky)/cholesky | solution.py:65
  455.2 5.1 all-to-all-start.8
  460.8 11.7 %cholesky.181 = f32[128,128]{1,0:T(8,128)S(1)} custom-call(f32[128,128]{1,0:T(8,128)S(1)} %convolution_subtract_fusion.4), custom_call_target="Cholesky" | custom-call | tf_op jit(solution)/shard_map/jit(cholesky)/cholesky | solution.py:65
  481.9 19.7 %custom-call.18 = f32[2,128,128]{1,2,0:T(8,128)S(1)} custom-call(f32[2,128,128]{2,1,0:T(8,128)S(1)} %get-tuple-element.21), custom_call_target="InvertDiagBlocksLowerTriangular" | custom-call | tf_op jit(solution)/shard_map/jit(_cho_solve)/triangular_solve | solution.py:66
  503.2 11.4 %reduce-scatter.5.cloned.1.call-done = f32[512,64]{0,1:T(8,128)} async-done(((f32[4096,64]{0,1:T(8,128)}), f32[512,64]{0,1:T(8,128)}) %reduce-scatter.5.cloned.1.call-update) | async-done | bytes 131088 | tf_op jit(solution)/shard_map/reduce_scatter | solution.py:51
  516.1 4.6 all-to-all-start.9
  521.0 5.7 %all-to-all-done.9 = f32[4,128,64]{1,2,0:T(8,128)S(1)} async-done(((f32[4,128,64]{1,2,0:T(8,128)}), f32[4,128,64]{1,2,0:T(8,128)S(1)}, u32[]{:S(2)}, u32[]{:S(2)}) %all-to-all-start.9) | async-done | bytes 131104 | tf_op jit(solution)/shard_map/all_to_all | solution.py:76
  549.1 5.2 all-to-all-done.13
  (135 shorter events, 110.0 us)
Async XLA Ops:
  8.0 19.7 %copy-start = (f32[512,64]{0,1:T(8,128)S(1)}, f32[512,64]{0,1:T(8,128)}, u32[]{:S(2)}) copy-start(f32[512,64]{0,1:T(8,128)} %param.16) | copy-start | bytes 393220
  8.0 165.9 %copy-start.1 = (f32[8,256]{1,0:T(8,128)S(1)}, f32[8,256]{1,0:T(8,128)}, u32[]{:S(2)}) copy-start(f32[8,256]{1,0:T(8,128)} %param.18) | copy-start | bytes 24580
  9.6 23.9 %all-to-all-start.3 = ((f32[4,128,64]{1,2,0:T(8,128)}), f32[4,128,64]{1,2,0:T(8,128)S(1)}, u32[]{:S(2)}, u32[]{:S(2)}) async-start(f32[4,128,64]{1,2,0:T(8,128)} %copy_bitcast_fusion.8), calls=%async_computation.4 | async-start | bytes 262144 | tf_op jit(solution)/shard_map/all_to_all | solution.py:111
  33.5 11.5 %all-to-all-start.4 = ((f32[4,128,64]{1,2,0:T(8,128)}), f32[4,128,64]{1,2,0:T(8,128)S(1)}, u32[]{:S(2)}, u32[]{:S(2)}) async-start(f32[4,128,64]{1,2,0:T(8,128)} %copy_bitcast_fusion.7), calls=%async_computation.5 | async-start | bytes 262144 | tf_op jit(solution)/shard_map/all_to_all | solution.py:109
  38.6 135.3 %all-reduce.4.cloned.1.call-start = ((), (), s32[]{:S(2)}) async-start(), calls=%async_computation.17 | async-start | bytes 524288 | tf_op jit(solution)/shard_map/psum | solution.py:61
  45.1 9.3 %all-to-all-start.5 = ((f32[4,128,64]{1,2,0:T(8,128)}), f32[4,128,64]{1,2,0:T(8,128)S(1)}, u32[]{:S(2)}, u32[]{:S(2)}) async-start(f32[4,128,64]{1,2,0:T(8,128)} %copy_bitcast_fusion.6), calls=%async_computation.6 | async-start | bytes 262144 | tf_op jit(solution)/shard_map/all_to_all | solution.py:110
  54.3 144.3 %all-to-all-start = ((bf16[4,512,64]{1,2,0:T(8,128)(2,1)}), bf16[4,512,64]{1,2,0:T(8,128)(2,1)S(1)}, u32[]{:S(2)}, u32[]{:S(2)}) async-start(bf16[4,512,64]{1,2,0:T(8,128)(2,1)} %copy.173), calls=%async_computation | async-start | bytes 524288 | tf_op jit(solution)/shard_map/all_to_all | solution.py:31
  203.5 18.1 %all-to-all-start.1 = ((f32[1,512,256]{1,0,2:T(1,128)}), f32[1,512,256]{1,0,2:T(1,128)S(1)}, u32[]{:S(2)}, u32[]{:S(2)}) async-start(f32[1,512,256]{1,0,2:T(1,128)} %copy.174), calls=%async_computation.1 | async-start | bytes 1048576 | tf_op jit(solution)/shard_map/all_to_all | solution.py:44
  207.1 54.6 %reduce-scatter.3.cloned.1.call-start = ((), (), s32[]{:S(2)}) async-start(), calls=%async_computation.16 | async-start | bytes 1179648 | tf_op jit(solution)/shard_map/reduce_scatter | solution.py:51
  263.2 10.5 %all-to-all-start.2 = ((f32[4,128,64]{1,2,0:T(8,128)}), f32[4,128,64]{1,2,0:T(8,128)S(1)}, u32[]{:S(2)}, u32[]{:S(2)}) async-start(f32[4,128,64]{1,2,0:T(8,128)} %copy_bitcast_fusion.9), calls=%async_computation.3 | async-start | bytes 262144 | tf_op jit(solution)/shard_map/all_to_all | solution.py:76
  273.7 9.2 %all-to-all-start.10 = ((f32[4,128,64]{1,2,0:T(8,128)}), f32[4,128,64]{1,2,0:T(8,128)S(1)}, u32[]{:S(2)}, u32[]{:S(2)}) async-start(f32[4,128,64]{1,2,0:T(8,128)} %copy_bitcast_fusion.4), calls=%async_computation.12 | async-start | bytes 262144 | tf_op jit(solution)/shard_map/all_to_all | solution.py:112
  277.1 133.4 %all-reduce.6.cloned.1.call-start = ((), (), s32[]{:S(2)}) async-start(), calls=%async_computation.19 | async-start | bytes 524288 | tf_op jit(solution)/shard_map/psum | solution.py:61
  283.8 129.1 %all-to-all-start.6 = ((f32[128,4,64]{0,2,1:T(8,128)}), f32[128,4,64]{0,2,1:T(8,128)S(1)}, u32[]{:S(2)}, u32[]{:S(2)}) async-start(f32[128,4,64]{0,2,1:T(8,128)} %bitcast.28), calls=%async_computation.7 | async-start | bytes 262144 | tf_op jit(solution)/shard_map/all_to_all | solution.py:85
  424.9 25.5 %all-to-all-start.7 = ((bf16[4,512,64]{1,2,0:T(8,128)(2,1)}), bf16[4,512,64]{1,2,0:T(8,128)(2,1)S(1)}, u32[]{:S(2)}, u32[]{:S(2)}) async-start(bf16[4,512,64]{1,2,0:T(8,128)(2,1)} %copy.192), calls=%async_computation.8 | async-start | bytes 524288 | tf_op jit(solution)/shard_map/all_to_all | solution.py:31
  455.2 20.0 %all-to-all-start.8 = ((f32[1,512,256]{1,0,2:T(1,128)}), f32[1,512,256]{1,0,2:T(1,128)S(1)}, u32[]{:S(2)}, u32[]{:S(2)}) async-start(f32[1,512,256]{1,0,2:T(1,128)} %copy.193), calls=%async_computation.9 | async-start | bytes 1048576 | tf_op jit(solution)/shard_map/all_to_all | solution.py:44
  460.3 54.2 %reduce-scatter.5.cloned.1.call-start = ((), (), s32[]{:S(2)}) async-start(), calls=%async_computation.18 | async-start | bytes 1179648 | tf_op jit(solution)/shard_map/reduce_scatter | solution.py:51
  516.1 10.5 %all-to-all-start.9 = ((f32[4,128,64]{1,2,0:T(8,128)}), f32[4,128,64]{1,2,0:T(8,128)S(1)}, u32[]{:S(2)}, u32[]{:S(2)}) async-start(f32[4,128,64]{1,2,0:T(8,128)} %copy_bitcast_fusion.5), calls=%async_computation.11 | async-start | bytes 262144 | tf_op jit(solution)/shard_map/all_to_all | solution.py:76
  526.6 9.2 %all-to-all-start.12 = ((f32[128,4,64]{0,2,1:T(8,128)}), f32[128,4,64]{0,2,1:T(8,128)S(1)}, u32[]{:S(2)}, u32[]{:S(2)}) async-start(f32[128,4,64]{0,2,1:T(8,128)} %bitcast.54), calls=%async_computation.14 | async-start | bytes 262144 | tf_op jit(solution)/shard_map/all_to_all | solution.py:86
  535.9 9.2 %all-to-all-start.11 = ((f32[128,4,64]{0,2,1:T(8,128)}), f32[128,4,64]{0,2,1:T(8,128)S(1)}, u32[]{:S(2)}, u32[]{:S(2)}) async-start(f32[128,4,64]{0,2,1:T(8,128)} %bitcast.52), calls=%async_computation.13 | async-start | bytes 262144 | tf_op jit(solution)/shard_map/all_to_all | solution.py:85
  545.1 9.2 %all-to-all-start.13 = ((f32[128,4,64]{0,2,1:T(8,128)}), f32[128,4,64]{0,2,1:T(8,128)S(1)}, u32[]{:S(2)}, u32[]{:S(2)}) async-start(f32[128,4,64]{0,2,1:T(8,128)} %bitcast.56), calls=%async_computation.15 | async-start | bytes 262144 | tf_op jit(solution)/shard_map/all_to_all | solution.py:86
Sparse Core Ops, SparseCore 0:
  44.9 128.9 all-reduce.3
  283.4 127.0 all-reduce.5
Sparse Core Ops, SparseCore 1:
  224.3 37.3 reduce-scatter.2
  477.9 36.6 reduce-scatter.4
where the time goes:
time: 572 us; the launch traced here: 563 us
  waiting for transfers between devices  302 us (53%)
  other arithmetic  113 us (20%)
  starting transfers between devices  57 us (10%)
  local copies, waits for them, and re-layouts  30.9 us (5%)
  between operations  20.2 us (4%)
  blocking collectives  19.8 us (3%)
  matrix products  19.7 us (3%)
    psum x2, waiting for transfers between devices, joint_gram(): total = lax.psum(local_gram, ('wide', 'narrow'))  239 us
    another operation x13, other arithmetic, joint_gram(): lower = jnp.linalg.cholesky(gram + penalty * identity)  68.5 us
    another operation x5, other arithmetic, joint_gram(): inverse = jax.scipy.linalg.cho_solve((lower, True), identity)  39.4 us
    reduce_scatter x2, waiting for transfers between devices, owner_sums(): lax.psum_scatter(placed.reshape(owned * lax.axis_size('wide'), width), 'w...  23.4 us
    all_gather x2, blocking collectives, fetch_rows(): portion = lax.all_gather(lowered, 'wide', axis=0, tiled=True)  19.8 us
  transfers between devices with their start and end apart: 18, of which 12 were waited for; matrix products, arithmetic and copies ran while one was open for 25% of the time, Pallas kernels for 0%

commit v1 on v0

--- a/solution.py
+++ b/solution.py
@@ -58,7 +58,7 @@
 
 def joint_gram(other_rows, time_factor):
     local_gram = jnp.dot(other_rows.T, other_rows, precision=lax.Precision.HIGHEST)
-    total = lax.psum(local_gram, ("wide", "narrow"))
+    total = lax.psum(lax.psum(local_gram, "wide"), "narrow")
     gram = total * jnp.dot(time_factor.T, time_factor, precision=lax.Precision.HIGHEST)
     penalty = jnp.trace(gram) / RANK
     identity = jnp.eye(RANK, dtype=jnp.float32)

time: 572 us -> 494 us (0.86)
  waiting for transfers between devices: 302 us -> 231 us
    psum x2 -> x4, waiting for transfers between devices: 239 us -> 167 us  [joint_gram(): total = lax.psum(lax.psum(local_gram, 'wide'), 'narrow')]
  transfers between devices with their start and end apart: 18 -> 20, of which waited for: 12 -> 14; matrix products, arithmetic and copies ran while one was open for 25% -> 30% of each run, Pallas kernels for 0% -> 0%
where the time goes in v1:
time: 494 us; the launch traced here: 489 us
  waiting for transfers between devices  231 us (47%)
  other arithmetic  113 us (23%)
  starting transfers between devices  57.6 us (12%)
  local copies, waits for them, and re-layouts  29.3 us (6%)
  matrix products  19.7 us (4%)
  blocking collectives  19 us (4%)
  between operations  18.9 us (4%)
    psum x4, waiting for transfers between devices, joint_gram(): total = lax.psum(lax.psum(local_gram, 'wide'), 'narrow')  167 us
    another operation x13, other arithmetic, joint_gram(): lower = jnp.linalg.cholesky(gram + penalty * identity)  68.7 us
    another operation x5, other arithmetic, joint_gram(): inverse = jax.scipy.linalg.cho_solve((lower, True), identity)  39.4 us
    reduce_scatter x2, waiting for transfers between devices, owner_sums(): lax.psum_scatter(placed.reshape(owned * lax.axis_size('wide'), width), 'w...  23.5 us
    all_gather x2, blocking collectives, fetch_rows(): portion = lax.all_gather(lowered, 'wide', axis=0, tiled=True)  19 us
    all_to_all x2, waiting for transfers between devices, update_rows(): lax.all_to_all(sums, 'narrow', split_axis=0, concat_axis=1, tiled=True)  11.3 us
  transfers between devices with their start and end apart: 20, of which 14 were waited for; matrix products, arithmetic and copies ran while one was open for 30% of the time, Pallas kernels for 0%

profile of v1, /device:TPU:0, one launch (start us, length us, event | category | flops | bytes accessed | tf_op | source)
XLA Modules:
  0.0 489.0 jit_solution(4375187541683312818)
XLA Ops:
  8.8 6.3 %all-to-all-start.3 = ((f32[4,128,64]{1,2,0:T(8,128)}), f32[4,128,64]{1,2,0:T(8,128)S(1)}, u32[]{:S(2)}, u32[]{:S(2)}) async-start(f32[4,128,64]{1,2,0:T(8,128)} %copy_bitcast_fusion.8), calls=%async_computation.4 | async-start | bytes 262144 | tf_op jit(solution)/shard_map/all_to_all | solution.py:111
  16.1 9.9 %all_gather.6 = bf16[4096,64]{0,1:T(8,128)(2,1)S(1)} all-gather(bf16[512,64]{0,1:T(8,128)(2,1)S(1)} %convert_element_type.70), channel_id=1, replica_groups=mesh['wide'=8,'narrow'=4] {'wide'}, dimensions={0}, use_global_device_ids=true | all-gather | bytes 589824 | tf_op jit(solution)/shard_map/all_gather | solution.py:22
  30.4 5.1 %all-to-all-start.4 = ((f32[4,128,64]{1,2,0:T(8,128)}), f32[4,128,64]{1,2,0:T(8,128)S(1)}, u32[]{:S(2)}, u32[]{:S(2)}) async-start(f32[4,128,64]{1,2,0:T(8,128)} %copy_bitcast_fusion.7), calls=%async_computation.5 | async-start | bytes 262144 | tf_op jit(solution)/shard_map/all_to_all | solution.py:109
  36.1 5.8 %all-to-all-done.4 = f32[4,128,64]{1,2,0:T(8,128)S(1)} async-done(((f32[4,128,64]{1,2,0:T(8,128)}), f32[4,128,64]{1,2,0:T(8,128)S(1)}, u32[]{:S(2)}, u32[]{:S(2)}) %all-to-all-start.4) | async-done | bytes 131104 | tf_op jit(solution)/shard_map/all_to_all | solution.py:109
  45.9 5.2 %all-to-all-done.5 = f32[4,128,64]{1,2,0:T(8,128)S(1)} async-done(((f32[4,128,64]{1,2,0:T(8,128)}), f32[4,128,64]{1,2,0:T(8,128)S(1)}, u32[]{:S(2)}, u32[]{:S(2)}) %all-to-all-start.5) | async-done | bytes 131104 | tf_op jit(solution)/shard_map/all_to_all | solution.py:110
  56.0 56.8 %all-reduce.6.cloned.1.call-done = f32[256,256]{0,1:T(8,128)} async-done(((f32[256,256]{0,1:T(8,128)}), f32[256,256]{0,1:T(8,128)}) %all-reduce.6.cloned.1.call-update) | async-done | bytes 262160 | tf_op jit(solution)/shard_map/psum | solution.py:61
  122.5 32.8 %all-reduce.8.cloned.1.call-done = f32[256,256]{0,1:T(8,128)} async-done(((f32[256,256]{0,1:T(8,128)}), f32[256,256]{0,1:T(8,128)}) %all-reduce.8.cloned.1.call-update) | async-done | bytes 262160 | tf_op jit(solution)/shard_map/psum | solution.py:61
  158.2 11.7 %cholesky.130 = f32[128,128]{1,0:T(8,128)S(1)} custom-call(f32[128,128]{1,0:T(8,128)S(1)} %cholesky.194), custom_call_target="Cholesky" | custom-call | tf_op jit(solution)/shard_map/jit(cholesky)/cholesky | solution.py:65
  169.9 9.8 %custom-call.15 = f32[1,128,128]{1,2,0:T(8,128)S(1)} custom-call(f32[1,128,128]{2,1,0:T(8,128)S(1)} %get-tuple-element.59), custom_call_target="InvertDiagBlocksLowerTriangular" | custom-call | tf_op jit(solution)/shard_map/jit(cholesky)/cholesky | solution.py:65
  180.2 11.7 %cholesky.147 = f32[128,128]{1,0:T(8,128)S(1)} custom-call(f32[128,128]{1,0:T(8,128)S(1)} %convolution_subtract_fusion.5), custom_call_target="Cholesky" | custom-call | tf_op jit(solution)/shard_map/jit(cholesky)/cholesky | solution.py:65
  201.2 19.7 %custom-call.16 = f32[2,128,128]{1,2,0:T(8,128)S(1)} custom-call(f32[2,128,128]{2,1,0:T(8,128)S(1)} %get-tuple-element.20), custom_call_target="InvertDiagBlocksLowerTriangular" | custom-call | tf_op jit(solution)/shard_map/jit(_cho_solve)/triangular_solve | solution.py:66
  222.5 11.0 %reduce-scatter.3.cloned.1.call-done = f32[512,64]{0,1:T(8,128)} async-done(((f32[4096,64]{0,1:T(8,128)}), f32[512,64]{0,1:T(8,128)}) %reduce-scatter.3.cloned.1.call-update) | async-done | bytes 131088 | tf_op jit(solution)/shard_map/reduce_scatter | solution.py:51
  239.9 5.7 %all-to-all-done.2 = f32[4,128,64]{1,2,0:T(8,128)S(1)} async-done(((f32[4,128,64]{1,2,0:T(8,128)}), f32[4,128,64]{1,2,0:T(8,128)S(1)}, u32[]{:S(2)}, u32[]{:S(2)}) %all-to-all-start.2) | async-done | bytes 131104 | tf_op jit(solution)/shard_map/all_to_all | solution.py:76
  260.3 55.7 %all-reduce.10.cloned.1.call-done = f32[256,256]{0,1:T(8,128)} async-done(((f32[256,256]{0,1:T(8,128)}), f32[256,256]{0,1:T(8,128)}) %all-reduce.10.cloned.1.call-update) | async-done | bytes 262160 | tf_op jit(solution)/shard_map/psum | solution.py:61
  316.7 9.2 %all_gather.7 = bf16[4096,64]{0,1:T(8,128)(2,1)S(1)} all-gather(bf16[512,64]{0,1:T(8,128)(2,1)S(1)} %get-tuple-element.40), channel_id=1, replica_groups=mesh['wide'=8,'narrow'=4] {'wide'}, dimensions={0}, use_global_device_ids=true | all-gather | bytes 589824 | tf_op jit(solution)/shard_map/all_gather | solution.py:22
  327.2 4.8 all-to-all-start.7
  331.9 21.5 %all-reduce.12.cloned.1.call-done = f32[256,256]{0,1:T(8,128)} async-done(((f32[256,256]{0,1:T(8,128)}), f32[256,256]{0,1:T(8,128)}) %all-reduce.12.cloned.1.call-update) | async-done | bytes 262160 | tf_op jit(solution)/shard_map/psum | solution.py:61
  356.0 11.7 %cholesky.164 = f32[128,128]{1,0:T(8,128)S(1)} custom-call(f32[128,128]{1,0:T(8,128)S(1)} %cholesky.197), custom_call_target="Cholesky" | custom-call | tf_op jit(solution)/shard_map/jit(cholesky)/cholesky | solution.py:65
  367.7 9.8 %custom-call.17 = f32[1,128,128]{1,2,0:T(8,128)S(1)} custom-call(f32[1,128,128]{2,1,0:T(8,128)S(1)} %get-tuple-element.55), custom_call_target="InvertDiagBlocksLowerTriangular" | custom-call | tf_op jit(solution)/shard_map/jit(cholesky)/cholesky | solution.py:65
  386.7 11.7 %cholesky.181 = f32[128,128]{1,0:T(8,128)S(1)} custom-call(f32[128,128]{1,0:T(8,128)S(1)} %convolution_subtract_fusion.4), custom_call_target="Cholesky" | custom-call | tf_op jit(solution)/shard_map/jit(cholesky)/cholesky | solution.py:65
  407.7 19.7 %custom-call.18 = f32[2,128,128]{1,2,0:T(8,128)S(1)} custom-call(f32[2,128,128]{2,1,0:T(8,128)S(1)} %get-tuple-element.21), custom_call_target="InvertDiagBlocksLowerTriangular" | custom-call | tf_op jit(solution)/shard_map/jit(_cho_solve)/triangular_solve | solution.py:66
  429.0 12.5 %reduce-scatter.5.cloned.1.call-done = f32[512,64]{0,1:T(8,128)} async-done(((f32[4096,64]{0,1:T(8,128)}), f32[512,64]{0,1:T(8,128)}) %reduce-scatter.5.cloned.1.call-update) | async-done | bytes 131088 | tf_op jit(solution)/shard_map/reduce_scatter | solution.py:51
  447.9 5.7 %all-to-all-done.9 = f32[4,128,64]{1,2,0:T(8,128)S(1)} async-done(((f32[4,128,64]{1,2,0:T(8,128)}), f32[4,128,64]{1,2,0:T(8,128)S(1)}, u32[]{:S(2)}, u32[]{:S(2)}) %all-to-all-start.9) | async-done | bytes 131104 | tf_op jit(solution)/shard_map/all_to_all | solution.py:76
  476.0 5.2 %all-to-all-done.13 = f32[128,4,64]{0,2,1:T(8,128)S(1)} async-done(((f32[128,4,64]{0,2,1:T(8,128)}), f32[128,4,64]{0,2,1:T(8,128)S(1)}, u32[]{:S(2)}, u32[]{:S(2)}) %all-to-all-start.13) | async-done | bytes 131104 | tf_op jit(solution)/shard_map/all_to_all | solution.py:86
  (145 shorter events, 118.7 us)
Async XLA Ops:
  7.2 22.5 %copy-start = (f32[512,64]{0,1:T(8,128)S(1)}, f32[512,64]{0,1:T(8,128)}, u32[]{:S(2)}) copy-start(f32[512,64]{0,1:T(8,128)} %param.16) | copy-start | bytes 393220
  7.2 28.3 %copy-start.1 = (f32[512,64]{0,1:T(8,128)S(1)}, f32[512,64]{0,1:T(8,128)}, u32[]{:S(2)}) copy-start(f32[512,64]{0,1:T(8,128)} %param.19) | copy-start | bytes 393220
  7.2 38.0 %copy-start.2 = (f32[512,64]{0,1:T(8,128)S(1)}, f32[512,64]{0,1:T(8,128)}, u32[]{:S(2)}) copy-start(f32[512,64]{0,1:T(8,128)} %param.20) | copy-start | bytes 393220
  7.2 105.6 %copy-start.3 = (f32[8,256]{1,0:T(8,128)S(1)}, f32[8,256]{1,0:T(8,128)}, u32[]{:S(2)}) copy-start(f32[8,256]{1,0:T(8,128)} %param.18) | copy-start | bytes 24580
  8.8 21.5 %all-to-all-start.3 = ((f32[4,128,64]{1,2,0:T(8,128)}), f32[4,128,64]{1,2,0:T(8,128)S(1)}, u32[]{:S(2)}, u32[]{:S(2)}) async-start(f32[4,128,64]{1,2,0:T(8,128)} %copy_bitcast_fusion.8), calls=%async_computation.4 | async-start | bytes 262144 | tf_op jit(solution)/shard_map/all_to_all | solution.py:111
  30.4 11.5 %all-to-all-start.4 = ((f32[4,128,64]{1,2,0:T(8,128)}), f32[4,128,64]{1,2,0:T(8,128)S(1)}, u32[]{:S(2)}, u32[]{:S(2)}) async-start(f32[4,128,64]{1,2,0:T(8,128)} %copy_bitcast_fusion.7), calls=%async_computation.5 | async-start | bytes 262144 | tf_op jit(solution)/shard_map/all_to_all | solution.py:109
  41.9 9.2 %all-to-all-start.5 = ((f32[4,128,64]{1,2,0:T(8,128)}), f32[4,128,64]{1,2,0:T(8,128)S(1)}, u32[]{:S(2)}, u32[]{:S(2)}) async-start(f32[4,128,64]{1,2,0:T(8,128)} %copy_bitcast_fusion.6), calls=%async_computation.6 | async-start | bytes 262144 | tf_op jit(solution)/shard_map/all_to_all | solution.py:110
  51.1 61.7 %all-to-all-start = ((bf16[4,512,64]{1,2,0:T(8,128)(2,1)}), bf16[4,512,64]{1,2,0:T(8,128)(2,1)S(1)}, u32[]{:S(2)}, u32[]{:S(2)}) async-start(bf16[4,512,64]{1,2,0:T(8,128)(2,1)} %copy.173), calls=%async_computation | async-start | bytes 524288 | tf_op jit(solution)/shard_map/all_to_all | solution.py:31
  54.5 58.2 %all-reduce.6.cloned.1.call-start = ((), (), s32[]{:S(2)}) async-start(), calls=%async_computation.17 | async-start | bytes 524288 | tf_op jit(solution)/shard_map/psum | solution.py:61
  55.7 99.6 %all-reduce.8.cloned.1.call-start = ((), (), s32[]{:S(2)}) async-start(), calls=%async_computation.18 | async-start | bytes 524288 | tf_op jit(solution)/shard_map/psum | solution.py:61
  117.6 76.4 %all-to-all-start.1 = ((f32[1,512,256]{1,0,2:T(1,128)}), f32[1,512,256]{1,0,2:T(1,128)S(1)}, u32[]{:S(2)}, u32[]{:S(2)}) async-start(f32[1,512,256]{1,0,2:T(1,128)} %copy.174), calls=%async_computation.1 | async-start | bytes 1048576 | tf_op jit(solution)/shard_map/all_to_all | solution.py:44
  122.2 111.2 %reduce-scatter.3.cloned.1.call-start = ((), (), s32[]{:S(2)}) async-start(), calls=%async_computation.16 | async-start | bytes 1179648 | tf_op jit(solution)/shard_map/reduce_scatter | solution.py:51
  235.0 10.5 %all-to-all-start.2 = ((f32[4,128,64]{1,2,0:T(8,128)}), f32[4,128,64]{1,2,0:T(8,128)S(1)}, u32[]{:S(2)}, u32[]{:S(2)}) async-start(f32[4,128,64]{1,2,0:T(8,128)} %copy_bitcast_fusion.9), calls=%async_computation.3 | async-start | bytes 262144 | tf_op jit(solution)/shard_map/all_to_all | solution.py:76
  245.5 9.2 %all-to-all-start.10 = ((f32[4,128,64]{1,2,0:T(8,128)}), f32[4,128,64]{1,2,0:T(8,128)S(1)}, u32[]{:S(2)}, u32[]{:S(2)}) async-start(f32[4,128,64]{1,2,0:T(8,128)} %copy_bitcast_fusion.4), calls=%async_computation.12 | async-start | bytes 262144 | tf_op jit(solution)/shard_map/all_to_all | solution.py:112
  254.8 61.3 %all-to-all-start.6 = ((f32[128,4,64]{0,2,1:T(8,128)}), f32[128,4,64]{0,2,1:T(8,128)S(1)}, u32[]{:S(2)}, u32[]{:S(2)}) async-start(f32[128,4,64]{0,2,1:T(8,128)} %bitcast.28), calls=%async_computation.7 | async-start | bytes 262144 | tf_op jit(solution)/shard_map/all_to_all | solution.py:85
  258.1 57.9 %all-reduce.10.cloned.1.call-start = ((), (), s32[]{:S(2)}) async-start(), calls=%async_computation.20 | async-start | bytes 524288 | tf_op jit(solution)/shard_map/psum | solution.py:61
  259.3 94.2 %all-reduce.12.cloned.1.call-start = ((), (), s32[]{:S(2)}) async-start(), calls=%async_computation.21 | async-start | bytes 524288 | tf_op jit(solution)/shard_map/psum | solution.py:61
  327.2 50.6 %all-to-all-start.7 = ((bf16[4,512,64]{1,2,0:T(8,128)(2,1)}), bf16[4,512,64]{1,2,0:T(8,128)(2,1)S(1)}, u32[]{:S(2)}, u32[]{:S(2)}) async-start(bf16[4,512,64]{1,2,0:T(8,128)(2,1)} %copy.192), calls=%async_computation.8 | async-start | bytes 524288 | tf_op jit(solution)/shard_map/all_to_all | solution.py:31
  382.7 18.5 %all-to-all-start.8 = ((f32[1,512,256]{1,0,2:T(1,128)}), f32[1,512,256]{1,0,2:T(1,128)S(1)}, u32[]{:S(2)}, u32[]{:S(2)}) async-start(f32[1,512,256]{1,0,2:T(1,128)} %copy.193), calls=%async_computation.9 | async-start | bytes 1048576 | tf_op jit(solution)/shard_map/all_to_all | solution.py:44
  386.2 55.3 %reduce-scatter.5.cloned.1.call-start = ((), (), s32[]{:S(2)}) async-start(), calls=%async_computation.19 | async-start | bytes 1179648 | tf_op jit(solution)/shard_map/reduce_scatter | solution.py:51
  443.0 10.5 %all-to-all-start.9 = ((f32[4,128,64]{1,2,0:T(8,128)}), f32[4,128,64]{1,2,0:T(8,128)S(1)}, u32[]{:S(2)}, u32[]{:S(2)}) async-start(f32[4,128,64]{1,2,0:T(8,128)} %copy_bitcast_fusion.5), calls=%async_computation.11 | async-start | bytes 262144 | tf_op jit(solution)/shard_map/all_to_all | solution.py:76
  453.6 9.2 %all-to-all-start.12 = ((f32[128,4,64]{0,2,1:T(8,128)}), f32[128,4,64]{0,2,1:T(8,128)S(1)}, u32[]{:S(2)}, u32[]{:S(2)}) async-start(f32[128,4,64]{0,2,1:T(8,128)} %bitcast.54), calls=%async_computation.14 | async-start | bytes 262144 | tf_op jit(solution)/shard_map/all_to_all | solution.py:86
  462.8 9.2 %all-to-all-start.11 = ((f32[128,4,64]{0,2,1:T(8,128)}), f32[128,4,64]{0,2,1:T(8,128)S(1)}, u32[]{:S(2)}, u32[]{:S(2)}) async-start(f32[128,4,64]{0,2,1:T(8,128)} %bitcast.52), calls=%async_computation.13 | async-start | bytes 262144 | tf_op jit(solution)/shard_map/all_to_all | solution.py:85
  472.0 9.2 %all-to-all-start.13 = ((f32[128,4,64]{0,2,1:T(8,128)}), f32[128,4,64]{0,2,1:T(8,128)S(1)}, u32[]{:S(2)}, u32[]{:S(2)}) async-start(f32[128,4,64]{0,2,1:T(8,128)} %bitcast.56), calls=%async_computation.15 | async-start | bytes 262144 | tf_op jit(solution)/shard_map/all_to_all | solution.py:86
Sparse Core Ops, SparseCore 0:
  58.4 54.3 all-reduce.5
  115.1 40.2 all-reduce.7
  197.4 36.0 reduce-scatter.2
  261.7 54.3 all-reduce.9
  318.2 35.2 all-reduce.11
  404.0 37.4 reduce-scatter.4
